TPU v7x, 32 devices: a whole 2x2x4 slice. The times are simulated.
32 devices in a mesh: parts: 2 (over x), chol: 16 (over z, y, core).
Axes of the slice: x: 2, y: 2, z: 4, core: 2. Of those that a mesh axis runs over, the one named last changes fastest.
Arguments:
- orbitals: float32 [32, 100, 1024], P(('parts', 'chol')), parts along dimension 0, may hold values from -6 to 6
- intersection_inv: float32 [32, 100, 100], P(('parts', 'chol')), parts along dimension 0, may hold values from -0.625 to 0.625
- factor_rows: bfloat16 [4096, 1024], P('chol'), may hold values from -0.1875 to 0.1875
- factor_rotated: bfloat16 [100, 4096], replicated, may hold values from -0.625 to 0.625
- factor_core: bfloat16 [1024, 4096], P('chol'), may hold values from -0.125 to 0.125
- fields: float32 [32, 1024], P('parts', 'chol'), parts along dimension 0, may hold values from -6 to 6
Outputs:
- propagated: float32 [32, 100, 1024], P(('parts', 'chol')), parts along dimension 0
- force_bias: float32 [32, 1024], P('parts', 'chol'), parts along dimension 0
There are 2 independent parts, one for each index of `parts`. A program takes and returns all parts, laid end to end along the dimension named above; an argument that names none is the same for every part. Nothing has to cross between parts.
All inputs are finite; a program needn't handle non-finite values.
Results may differ from a plain program's by a relative error of at most 0.0091.
Values may be sent and summed in bfloat16 or wider, within the bound.
A program may use at most 64 MiB of HBM per device.

v0:
```python
import jax
import jax.numpy as jnp
from jax import lax
from jax.sharding import PartitionSpec as P

TAYLOR = 4


def density_one(half_green, all_rows, factor_rotated):
    projected = lax.dot_general(
        half_green, all_rows, (((1,), (1,)), ((), ())), preferred_element_type=jnp.float32
    )
    return jnp.sum(factor_rotated.astype(jnp.float32) * projected, axis=0).astype(jnp.bfloat16)


def propagate_one(orbital, potential, all_rows):
    total = orbital
    term = orbital
    for order in range(1, TAYLOR + 1):
        summed = lax.dot_general(
            term.astype(jnp.bfloat16),
            all_rows,
            (((1,), (1,)), ((), ())),
            preferred_element_type=jnp.float32,
        )
        scaled = (summed * potential[None, :] / order).astype(jnp.bfloat16)
        term = jnp.dot(scaled, all_rows, preferred_element_type=jnp.float32)
        total = total + term
    return total


def on_device(orbitals, intersection_inv, factor_rows, factor_rotated, factor_core, fields):
    walker_count = orbitals.shape[0]
    half_green = jnp.einsum(
        "wij,wjm->wim", intersection_inv, orbitals, precision=lax.Precision.HIGHEST
    ).astype(jnp.bfloat16)
    all_rows = lax.all_gather(factor_rows, "chol", axis=0, tiled=True)
    own_density = lax.map(lambda item: density_one(item, all_rows, factor_rotated), half_green)
    density = lax.all_gather(own_density, "chol", axis=0, tiled=True)
    force_bias = lax.dot_general(
        density, factor_core, (((1,), (1,)), ((), ())), preferred_element_type=jnp.float32
    )
    shifted = (fields - force_bias).astype(jnp.bfloat16)
    partial_sum = jnp.dot(shifted, factor_core, preferred_element_type=jnp.float32)
    summed_all = lax.psum(partial_sum, "chol")
    potential = lax.dynamic_slice_in_dim(
        summed_all, lax.axis_index("chol") * walker_count, walker_count, 0
    )
    propagated = lax.map(
        lambda pair: propagate_one(pair[0], pair[1], all_rows), (orbitals, potential)
    )
    return (propagated, force_bias)


def solution(mesh):
    in_specs = (
        P(("parts", "chol"), None, None),
        P(("parts", "chol"), None, None),
        P("chol", None),
        P(),
        P("chol", None),
        P("parts", "chol"),
    )
    out_specs = (P(("parts", "chol"), None, None), P("parts", "chol"))
    return jax.shard_map(
        on_device, mesh=mesh, in_specs=in_specs, out_specs=out_specs, check_vma=False
    )
```

profile of v0, /device:TPU:0, one launch (start us, length us, event | category | flops | bytes accessed | tf_op | source)
XLA Modules:
  0.0 249.2 jit_solution(8666170632495442712)
XLA Ops:
  7.2 0.0 copy-start
  7.2 0.0 copy-start.1
  7.2 0.0 copy-start.3
  7.2 0.0 all-gather.3.cloned.1.call-start
  7.2 0.7 all-gather.3.cloned.1.call-update
  7.9 0.0 all-reduce.2.cloned.1.call-start
  8.0 1.6 convolution_convert_fusion
  9.6 77.7 %all-gather.3.cloned.1.call-done = bf16[4096,1024]{1,0:T(8,128)(2,1)} async-done(((bf16[256,1024]{1,0:T(8,128)(2,1)}), bf16[4096,1024]{1,0:T(8,128)(2,1)}) %all-gather.3.cloned.1.call-update) | async-done | bytes 8388624 | tf_op jit(solution)/shard_map/all_gather | solution.py:37
  87.2 6.3 %fusion.7 = bf16[4096]{0:T(1024)(128)(2,1)S(1)} fusion(bf16[100,1024]{1,0:T(8,128)(2,1)S(1)} %convolution_convert_fusion, bf16[4096,1024]{1,0:T(8,128)(2,1)} %all-gather.3.cloned.1.call-done, bf16[100,4096]{1,0:T(8,128)(2,1)} %param.9), kind=kOutput, calls=%fused_computation.12 | convolution fusion | flops 840085504 | bytes 9420800 | tf_op jit(solution)/shard_map/while/body/eval_jaxpr/dot_general | solution.py:10
  93.5 19.5 %all-gather = bf16[65536]{0:T(1024)(128)(2,1)S(1)} all-gather(bf16[4096]{0:T(1024)(128)(2,1)S(1)} %fusion.7), channel_id=2, replica_groups=mesh['parts'=2,'chol'=16] {'chol'}, dimensions={0}, use_global_device_ids=true | all-gather | bytes 139264 | tf_op jit(solution)/shard_map/all_gather | solution.py:39
  113.0 0.1 reshape.20
  113.1 0.0 copy-done
  113.1 0.2 fusion.28
  113.3 0.0 copy-done.3
  113.3 0.0 copy-start.2
  113.3 0.9 fusion.24
  114.2 0.0 all-reduce.2.cloned.1.call-update
  114.3 87.1 %all-reduce.2.cloned.1.call-done = f32[16,4096]{1,0:T(8,128)} async-done(((f32[16,4096]{1,0:T(8,128)}), f32[16,4096]{1,0:T(8,128)}) %all-reduce.2.cloned.1.call-update) | async-done | bytes 262160 | tf_op jit(solution)/shard_map/psum | solution.py:45
  201.4 0.9 constant_dynamic-slice_fusion
  202.3 0.0 copy-done.1
  202.3 9.7 %fusion.11 = f32[100,1024]{1,0:T(8,128)S(1)} fusion(bf16[4096,1024]{1,0:T(8,128)(2,1)} %all-gather.3.cloned.1.call-done, f32[4096]{0:T(1024)S(1)} %bitcast.32, f32[1,100,1024]{2,0,1:T(1,128)S(1)} %copy-done.1), kind=kOutput, calls=%fused_computation.18 | convolution fusion | flops 1678540800 | bytes 9224192 | tf_op jit(solution)/shard_map/while/body/eval_jaxpr/dot_general | solution.py:27
  212.0 0.0 copy-done.2
  212.0 9.7 %fusion.10 = f32[100,1024]{1,0:T(8,128)S(1)} fusion(bf16[4096,1024]{1,0:T(8,128)(2,1)} %all-gather.3.cloned.1.call-done, f32[4096]{0:T(1024)S(1)} %bitcast.33, f32[100,1024]{1,0:T(8,128)S(1)} %fusion.11), kind=kOutput, calls=%fused_computation.17 | convolution fusion | flops 1679052800 | bytes 9224192 | tf_op jit(solution)/shard_map/while/body/eval_jaxpr/dot_general | solution.py:27
  221.7 9.7 %fusion.9 = f32[100,1024]{1,0:T(8,128)S(1)} fusion(bf16[4096,1024]{1,0:T(8,128)(2,1)} %all-gather.3.cloned.1.call-done, f32[4096]{0:T(1024)S(1)} %bitcast.34, f32[100,1024]{1,0:T(8,128)S(1)} %fusion.10), kind=kOutput, calls=%fused_computation.16 | convolution fusion | flops 1679052800 | bytes 9224192 | tf_op jit(solution)/shard_map/while/body/eval_jaxpr/dot_general | solution.py:27
  231.5 9.7 %fusion.8 = f32[1,100,1024]{2,1,0:T(8,128)S(1)} fusion(bf16[4096,1024]{1,0:T(8,128)(2,1)} %all-gather.3.cloned.1.call-done, f32[4096]{0:T(1024)S(1)} %bitcast.35, f32[100,1024]{1,0:T(8,128)S(1)} %fusion.9, f32[100,1024]{1,0:T(8,128)S(1)} %fusion.10, f32[100,1024]{1,0:T(8,128)S(1)} %fusion.11, f32[1,100,1024]{2,0,1:T(1,128)S(1)} %copy-done.1), kind=kOutput, calls=%fused_computation.14 | convolution fusion | flops 1679462400 | bytes 10452992 | tf_op jit(solution)/shard_map/while/body/eval_jaxpr/dot_general | solution.py:27
  241.2 1.2 copy.9
Async XLA Ops:
  7.2 105.9 %copy-start = (bf16[64,4096]{1,0:T(8,128)(2,1)S(1)}, bf16[64,4096]{1,0:T(8,128)(2,1)}, u32[]{:S(2)}) copy-start(bf16[64,4096]{1,0:T(8,128)(2,1)} %param.10) | copy-start | bytes 1572868
  7.2 195.2 %copy-start.1 = (f32[1,100,1024]{2,0,1:T(1,128)S(1)}, f32[1,100,1024]{2,0,1:T(1,128)}, u32[]{:S(2)}) copy-start(f32[1,100,1024]{2,0,1:T(1,128)} %param.6) | copy-start | bytes 1228804
  7.2 106.1 %copy-start.3 = (f32[16,64]{1,0:T(8,128)S(1)}, f32[16,64]{1,0:T(8,128)}, u32[]{:S(2)}) copy-start(f32[16,64]{1,0:T(8,128)} %param.11) | copy-start | bytes 12292
  7.2 80.0 %all-gather.3.cloned.1.call-start = ((), (), s32[]{:S(2)}) async-start(), calls=%async_computation | async-start | bytes 8912896 | tf_op jit(solution)/shard_map/all_gather | solution.py:37
  7.9 193.5 %all-reduce.2.cloned.1.call-start = ((), (), s32[]{:S(2)}) async-start(), calls=%async_computation.1 | async-start | bytes 524288 | tf_op jit(solution)/shard_map/psum | solution.py:45
  113.3 98.7 %copy-start.2 = (f32[16,64]{1,0:T(8,128)}, f32[16,64]{1,0:T(8,128)S(1)}, u32[]{:S(2)}) copy-start(f32[16,64]{1,0:T(8,128)S(1)} %fusion.28) | copy-start | bytes 12292
Sparse Core Ops, SparseCore 0:
  10.2 77.0 all-gather.2
  114.4 86.9 all-reduce.1
where the time goes:
time: 249 us
  waiting for transfers between devices  166 us (67%)
  matrix products  47.9 us (19%)
  blocking collectives  19.5 us (8%)
  between operations  14.1 us (6%)
    psum x1, waiting for transfers between devices, on_device(): summed_all = lax.psum(partial_sum, 'chol')  87.1 us
    all_gather x1, waiting for transfers between devices, on_device(): all_rows = lax.all_gather(factor_rows, 'chol', axis=0, tiled=True)  77.7 us
    dot_general x4, matrix products, propagate_one(): term = jnp.dot(scaled, all_rows, preferred_element_type=jnp.float32)  38.9 us
    all_gather x1, blocking collectives, on_device(): density = lax.all_gather(own_density, 'chol', axis=0, tiled=True)  19.5 us
    dot_general x1, matrix products, density_one(): lax.dot_general(half_green, all_rows, (((1,), (1,)), ((), ())), preferred...  6.26 us
  transfers between devices with their start and end apart: 2, of which 2 were waited for; matrix products, arithmetic and copies ran while one was open for 1% of the time, Pallas kernels for 0%

commit v1 on v0

--- a/solution.py
+++ b/solution.py
@@ -42,7 +42,10 @@
     )
     shifted = (fields - force_bias).astype(jnp.bfloat16)
     partial_sum = jnp.dot(shifted, factor_core, preferred_element_type=jnp.float32)
-    summed_all = lax.psum(partial_sum, "chol")
+    size, summed_all = (lax.axis_size("chol"), partial_sum)
+    for reach in [1 << k for k in range(size.bit_length() - 1)]:
+        pairs = [(i, i ^ reach) for i in range(size)]
+        summed_all = summed_all + lax.ppermute(summed_all, "chol", pairs)
     potential = lax.dynamic_slice_in_dim(
         summed_all, lax.axis_index("chol") * walker_count, walker_count, 0
     )

time: 249 us -> 192 us (0.77)
  waiting for transfers between devices: 166 us -> 109 us
    psum x1 -> x0, waiting for transfers between devices: 87.1 us -> none  [on_device(): summed_all = lax.psum(partial_sum, 'chol')]
    ppermute x0 -> x4, waiting for transfers between devices: none -> 30.6 us  [on_device(): summed_all = summed_all + lax.ppermute(summed_all, 'chol', pairs)]
  transfers between devices with their start and end apart: 2 -> 5, of which waited for: 2 -> 5; matrix products, arithmetic and copies ran while one was open for 1% -> 1% of each run, Pallas kernels for 0% -> 0%
where the time goes in v1:
time: 192 us
  waiting for transfers between devices  109 us (57%)
  matrix products  47.1 us (25%)
  blocking collectives  19.5 us (10%)
  between operations  14.1 us (7%)
    all_gather x1, waiting for transfers between devices, on_device(): all_rows = lax.all_gather(factor_rows, 'chol', axis=0, tiled=True)  77.7 us
    dot_general x4, matrix products, propagate_one(): term = jnp.dot(scaled, all_rows, preferred_element_type=jnp.float32)  38.8 us
    ppermute x4, waiting for transfers between devices, on_device(): summed_all = summed_all + lax.ppermute(summed_all, 'chol', pairs)  30.6 us
    all_gather x1, blocking collectives, on_device(): density = lax.all_gather(own_density, 'chol', axis=0, tiled=True)  19.5 us
    dot_general x1, matrix products, density_one(): lax.dot_general(half_green, all_rows, (((1,), (1,)), ((), ())), preferred...  6.26 us
  transfers between devices with their start and end apart: 5, of which 5 were waited for; matrix products, arithmetic and copies ran while one was open for 1% of the time, Pallas kernels for 0%

profile of v1, /device:TPU:0, one launch (start us, length us, event | category | flops | bytes accessed | tf_op | source)
XLA Modules:
  0.0 191.9 jit_solution(5680352916425631144)
XLA Ops:
  7.2 0.0 copy-start
  7.2 0.0 copy-start.1
  7.2 0.0 copy-start.3
  7.2 0.0 all-gather.3.cloned.1.call-start
  7.2 0.7 all-gather.3.cloned.1.call-update
  7.9 1.6 convolution_convert_fusion
  9.5 77.7 %all-gather.3.cloned.1.call-done = bf16[4096,1024]{1,0:T(8,128)(2,1)} async-done(((bf16[256,1024]{1,0:T(8,128)(2,1)}), bf16[4096,1024]{1,0:T(8,128)(2,1)}) %all-gather.3.cloned.1.call-update) | async-done | bytes 8388624 | tf_op jit(solution)/shard_map/all_gather | solution.py:37
  87.2 6.3 %fusion.7 = bf16[4096]{0:T(1024)(128)(2,1)S(1)} fusion(bf16[100,1024]{1,0:T(8,128)(2,1)S(1)} %convolution_convert_fusion, bf16[4096,1024]{1,0:T(8,128)(2,1)} %all-gather.3.cloned.1.call-done, bf16[100,4096]{1,0:T(8,128)(2,1)} %param.9), kind=kOutput, calls=%fused_computation.12 | convolution fusion | flops 840085504 | bytes 9420800 | tf_op jit(solution)/shard_map/while/body/eval_jaxpr/dot_general | solution.py:10
  93.5 19.5 %all-gather = bf16[65536]{0:T(1024)(128)(2,1)S(1)} all-gather(bf16[4096]{0:T(1024)(128)(2,1)S(1)} %fusion.7), channel_id=2, replica_groups=mesh['parts'=2,'chol'=16] {'chol'}, dimensions={0}, use_global_device_ids=true | all-gather | bytes 139264 | tf_op jit(solution)/shard_map/all_gather | solution.py:39
  113.0 0.1 reshape.20
  113.1 0.0 copy-done
  113.1 0.2 fusion.28
  113.3 0.0 copy-done.3
  113.3 0.0 copy-start.2
  113.3 0.2 fusion.24
  113.5 0.4 collective-permute-start
  113.9 1.2 collective-permute-done
  115.2 0.2 collective-permute-start.1
  115.4 8.4 %collective-permute-done.1 = f32[16,4096]{1,0:T(8,128)S(1)} collective-permute-done((f32[16,4096]{1,0:T(8,128)S(1)}, f32[16,4096]{1,0:T(8,128)S(1)}, u32[]{:S(2)}, u32[]{:S(2)}) %collective-permute-start.1) | collective-permute-done | bytes 262176 | tf_op jit(solution)/shard_map/ppermute | solution.py:48
  123.8 0.1 collective-permute-start.2
  123.9 7.7 %collective-permute-done.2 = f32[16,4096]{1,0:T(8,128)S(1)} collective-permute-done((f32[16,4096]{1,0:T(8,128)S(1)}, f32[16,4096]{1,0:T(8,128)S(1)}, u32[]{:S(2)}, u32[]{:S(2)}) %collective-permute-start.2) | collective-permute-done | bytes 262176 | tf_op jit(solution)/shard_map/ppermute | solution.py:48
  131.6 0.1 collective-permute-start.3
  131.7 13.3 %collective-permute-done.3 = f32[16,4096]{1,0:T(8,128)S(1)} collective-permute-done((f32[16,4096]{1,0:T(8,128)S(1)}, f32[16,4096]{1,0:T(8,128)S(1)}, u32[]{:S(2)}, u32[]{:S(2)}) %collective-permute-start.3) | collective-permute-done | bytes 262176 | tf_op jit(solution)/shard_map/ppermute | solution.py:48
  145.1 0.0 copy-done.1
  145.1 9.7 %fusion.11 = f32[100,1024]{1,0:T(8,128)S(1)} fusion(bf16[4096,1024]{1,0:T(8,128)(2,1)} %all-gather.3.cloned.1.call-done, f32[4096]{0:T(1024)S(1)} %bitcast.32, f32[1,100,1024]{2,0,1:T(1,128)S(1)} %copy-done.1), kind=kOutput, calls=%fused_computation.18 | convolution fusion | flops 1678540800 | bytes 9224192 | tf_op jit(solution)/shard_map/while/body/eval_jaxpr/dot_general | solution.py:27
  154.7 0.0 copy-done.2
  154.8 9.7 %fusion.10 = f32[100,1024]{1,0:T(8,128)S(1)} fusion(bf16[4096,1024]{1,0:T(8,128)(2,1)} %all-gather.3.cloned.1.call-done, f32[4096]{0:T(1024)S(1)} %bitcast.33, f32[100,1024]{1,0:T(8,128)S(1)} %fusion.11), kind=kOutput, calls=%fused_computation.17 | convolution fusion | flops 1679052800 | bytes 9224192 | tf_op jit(solution)/shard_map/while/body/eval_jaxpr/dot_general | solution.py:27
  164.4 9.7 %fusion.9 = f32[100,1024]{1,0:T(8,128)S(1)} fusion(bf16[4096,1024]{1,0:T(8,128)(2,1)} %all-gather.3.cloned.1.call-done, f32[4096]{0:T(1024)S(1)} %bitcast.34, f32[100,1024]{1,0:T(8,128)S(1)} %fusion.10), kind=kOutput, calls=%fused_computation.16 | convolution fusion | flops 1679052800 | bytes 9224192 | tf_op jit(solution)/shard_map/while/body/eval_jaxpr/dot_general | solution.py:27
  174.2 9.7 %fusion.8 = f32[1,100,1024]{2,1,0:T(8,128)S(1)} fusion(bf16[4096,1024]{1,0:T(8,128)(2,1)} %all-gather.3.cloned.1.call-done, f32[4096]{0:T(1024)S(1)} %bitcast.35, f32[100,1024]{1,0:T(8,128)S(1)} %fusion.9, f32[100,1024]{1,0:T(8,128)S(1)} %fusion.10, f32[100,1024]{1,0:T(8,128)S(1)} %fusion.11, f32[1,100,1024]{2,0,1:T(1,128)S(1)} %copy-done.1), kind=kOutput, calls=%fused_computation.14 | convolution fusion | flops 1679462400 | bytes 10452992 | tf_op jit(solution)/shard_map/while/body/eval_jaxpr/dot_general | solution.py:27
  183.9 1.2 copy.9
  (4 shorter events, 0.1 us)
Async XLA Ops:
  7.2 105.9 %copy-start = (bf16[64,4096]{1,0:T(8,128)(2,1)S(1)}, bf16[64,4096]{1,0:T(8,128)(2,1)}, u32[]{:S(2)}) copy-start(bf16[64,4096]{1,0:T(8,128)(2,1)} %param.10) | copy-start | bytes 1572868
  7.2 137.9 %copy-start.1 = (f32[1,100,1024]{2,0,1:T(1,128)S(1)}, f32[1,100,1024]{2,0,1:T(1,128)}, u32[]{:S(2)}) copy-start(f32[1,100,1024]{2,0,1:T(1,128)} %param.6) | copy-start | bytes 1228804
  7.2 106.1 %copy-start.3 = (f32[16,64]{1,0:T(8,128)S(1)}, f32[16,64]{1,0:T(8,128)}, u32[]{:S(2)}) copy-start(f32[16,64]{1,0:T(8,128)} %param.11) | copy-start | bytes 12292
  7.2 80.0 %all-gather.3.cloned.1.call-start = ((), (), s32[]{:S(2)}) async-start(), calls=%async_computation | async-start | bytes 8912896 | tf_op jit(solution)/shard_map/all_gather | solution.py:37
  113.3 41.4 %copy-start.2 = (f32[16,64]{1,0:T(8,128)}, f32[16,64]{1,0:T(8,128)S(1)}, u32[]{:S(2)}) copy-start(f32[16,64]{1,0:T(8,128)S(1)} %fusion.28) | copy-start | bytes 12292
  113.5 1.6 collective-permute-start
  115.2 8.6 %collective-permute-start.1 = (f32[16,4096]{1,0:T(8,128)S(1)}, f32[16,4096]{1,0:T(8,128)S(1)}, u32[]{:S(2)}, u32[]{:S(2)}) collective-permute-start(f32[16,4096]{1,0:T(8,128)S(1)} %add.35), channel_id=1, source_target_pairs={{0,2},{1,3},{2,0},{3,1},{4,6},{5,7},{6,4},{7,5},{8,10},{9,11},{10,... | collective-permute-start | bytes 786440 | tf_op jit(solution)/shard_map/ppermute | solution.py:48
  123.8 7.8 %collective-permute-start.2 = (f32[16,4096]{1,0:T(8,128)S(1)}, f32[16,4096]{1,0:T(8,128)S(1)}, u32[]{:S(2)}, u32[]{:S(2)}) collective-permute-start(f32[16,4096]{1,0:T(8,128)S(1)} %add.36), channel_id=1, source_target_pairs={{0,4},{1,5},{2,6},{3,7},{4,0},{5,1},{6,2},{7,3},{8,12},{9,13},{10,... | collective-permute-start | bytes 786440 | tf_op jit(solution)/shard_map/ppermute | solution.py:48
  131.6 13.4 %collective-permute-start.3 = (f32[16,4096]{1,0:T(8,128)S(1)}, f32[16,4096]{1,0:T(8,128)S(1)}, u32[]{:S(2)}, u32[]{:S(2)}) collective-permute-start(f32[16,4096]{1,0:T(8,128)S(1)} %add.37), channel_id=1, source_target_pairs={{0,8},{1,9},{2,10},{3,11},{4,12},{5,13},{6,14},{7,15},{8,0},{9,1},... | collective-permute-start | bytes 786440 | tf_op jit(solution)/shard_map/ppermute | solution.py:48
Sparse Core Ops, SparseCore 0:
  10.2 77.0 all-gather.2
